TPU v7x, 512 devices: a whole 4x4x16 slice. The times are simulated.
512 devices in a mesh: dp: 64 (over z, y), sub: 8 (over x, core).
Axes of the slice: x: 4, y: 4, z: 16, core: 2. Of those that a mesh axis runs over, the one named last changes fastest.
Arguments:
- embeddings: bfloat16 [524288, 1024], P(('dp', 'sub')), may hold values from -6 to 6
- cluster_of: int32 [524288], P(('dp', 'sub')), may hold values from 0 to 1087, as said below
Outputs:
- density: float32 [524288], P(('dp', 'sub'))
Inputs may be any that keep to these rules, and one draw needn't show every extreme that they name: `cluster_of`: A cluster c < 2 * 512 is held whole by the device of dp index (c // 2) // 8 and sub index (c // 2) % 8; a cluster c >= 2 * 512 is spread over the sub devices of dp index (c - 2 * 512). Of one device's rows exactly 896 lie in whole-held clusters and 128 in spread ones. At most 3 of one device's rows lie in the whole-held clusters of one device; one device gets exactly 3 such rows from every device. At most 4 of one device's rows lie in the spread clusters of one dp index; one dp index gets exactly 4 such rows from every device.
All inputs are finite; a program needn't handle non-finite values.
Results may differ from a plain program's by a relative error of at most 0.0005.
The roundings to bfloat16 on the way count: a program that leaves them out, or rounds other values in their place, can miss the bound.
Values may be sent and summed in bfloat16 or wider, within the bound.
A program may use at most 64 MiB of HBM per device.

v0:
```python
import jax
import jax.numpy as jnp
from jax import lax
from jax.sharding import PartitionSpec as P

SC = 2
LC = 1


kernel_scale = 32.0


def unit_norm(values):
    floats = values.astype(jnp.float32)
    scaled = floats * lax.rsqrt(jnp.sum(floats * floats, axis=1, keepdims=True) + 1e-06)
    return scaled.astype(jnp.bfloat16)


def pair_terms(left_rows, left_ids, left_place, right_rows, right_ids, right_place):
    similar = lax.dot_general(
        left_rows, right_rows, (((1,), (1,)), ((), ())), preferred_element_type=jnp.float32
    )
    same_cluster = (left_ids[:, None] == right_ids[None, :]) & (left_ids[:, None] >= 0)
    keep_pair = same_cluster & (left_place[:, None] != right_place[None, :])
    weights = jnp.where(keep_pair, jnp.exp(kernel_scale * similar), 0.0)
    return (weights, same_cluster.astype(jnp.float32))


def rank_within(labels):
    length = labels.shape[0]
    places = jnp.arange(length, dtype=jnp.int32)
    earlier = places[None, :] < places[:, None]
    matches = (labels[:, None] == labels[None, :]) & earlier
    return jnp.sum(matches.astype(jnp.int32), axis=1)


def finish(kernel_mass, members, labels):
    return jnp.where(labels >= 0, kernel_mass / jnp.maximum(members, 1.0), 0.0)


def local(embeddings, cluster_of):
    dp_count = lax.axis_size("dp")
    sub_count = lax.axis_size("sub")
    device_count = dp_count * sub_count
    local_rows = embeddings.shape[0]
    feature_width = embeddings.shape[1]
    spread_count = local_rows // 8
    planned_count = local_rows - spread_count
    small_cap = max(2, (3 * planned_count + 2 * device_count - 1) // (2 * device_count))
    large_cap = max(2, (2 * spread_count + dp_count - 1) // dp_count)
    unit_rows = unit_norm(embeddings)
    whole_count = SC * device_count
    planned = cluster_of < whole_count
    holder_of = cluster_of // SC
    owners = jnp.where(planned, holder_of // sub_count, (cluster_of - whole_count) // LC)
    tile_of = jnp.where(planned, holder_of % sub_count, -1)
    target = owners * sub_count + tile_of
    small_label = jnp.where(planned, target, -1)
    large_label = jnp.where(planned, -1, owners)
    small_slot = jnp.where(
        planned, target * small_cap + rank_within(small_label), device_count * small_cap
    )
    large_slot = jnp.where(
        planned, dp_count * large_cap, owners * large_cap + rank_within(large_label)
    )
    small_send = (
        jnp.zeros((device_count * small_cap, feature_width), jnp.bfloat16)
        .at[small_slot]
        .set(unit_rows, mode="drop")
    )
    small_send = small_send.reshape(dp_count, sub_count, small_cap, feature_width)
    small_tags = (
        jnp.full((device_count * small_cap,), -1, jnp.int32)
        .at[small_slot]
        .set(cluster_of, mode="drop")
    )
    small_tags = small_tags.reshape(dp_count, sub_count, small_cap)
    large_send = (
        jnp.zeros((dp_count * large_cap, feature_width), jnp.bfloat16)
        .at[large_slot]
        .set(unit_rows, mode="drop")
    )
    large_send = large_send.reshape(dp_count, large_cap, feature_width)
    large_tags = (
        jnp.full((dp_count * large_cap,), -1, jnp.int32).at[large_slot].set(cluster_of, mode="drop")
    )
    large_tags = large_tags.reshape(dp_count, large_cap)
    got_rows, got_tags = (
        lax.all_to_all(
            lax.all_to_all(small_send, "dp", split_axis=0, concat_axis=0, tiled=True),
            "sub",
            split_axis=1,
            concat_axis=1,
            tiled=True,
        ),
        lax.all_to_all(
            lax.all_to_all(small_tags, "dp", split_axis=0, concat_axis=0, tiled=True),
            "sub",
            split_axis=1,
            concat_axis=1,
            tiled=True,
        ),
    )
    got_large, got_large_tags = (
        lax.all_to_all(large_send, "dp", split_axis=0, concat_axis=0, tiled=True),
        lax.all_to_all(large_tags, "dp", split_axis=0, concat_axis=0, tiled=True),
    )
    planned_flat = got_rows.reshape(-1, feature_width)
    planned_ids = got_tags.reshape(-1)
    slot_total = planned_flat.shape[0]
    block_size = 512
    all_places = jnp.arange(slot_total, dtype=jnp.int32)

    def planned_block(block_index):
        block_start = block_index * block_size
        part_rows = lax.dynamic_slice_in_dim(planned_flat, block_start, block_size, 0)
        part_ids = lax.dynamic_slice_in_dim(planned_ids, block_start, block_size, 0)
        part_places = block_start + jnp.arange(block_size, dtype=jnp.int32)
        weights, same_cluster = pair_terms(
            part_rows, part_ids, part_places, planned_flat, planned_ids, all_places
        )
        return finish(jnp.sum(weights, axis=1), jnp.sum(same_cluster, axis=1), part_ids)

    planned_density = lax.map(planned_block, jnp.arange(slot_total // block_size, dtype=jnp.int32))
    planned_density = planned_density.reshape(dp_count, sub_count, small_cap)
    spread_flat = got_large.reshape(-1, feature_width)
    spread_ids = got_large_tags.reshape(-1)
    spread_total = spread_flat.shape[0]
    places = jnp.arange(spread_total, dtype=jnp.int32)
    my_places = lax.axis_index("sub") * spread_total + places
    piece_rows = lax.all_gather(spread_flat, "sub", axis=0, tiled=True)
    piece_ids = lax.all_gather(spread_ids, "sub", axis=0, tiled=True)
    piece_places = jnp.arange(piece_rows.shape[0], dtype=jnp.int32)
    weights, same_cluster = pair_terms(
        spread_flat, spread_ids, my_places, piece_rows, piece_ids, piece_places
    )
    kernel_mass = jnp.sum(weights, axis=1)
    members = jnp.sum(same_cluster, axis=1)
    spread_density = finish(kernel_mass, members, spread_ids).reshape(dp_count, large_cap)
    back_planned = lax.all_to_all(
        lax.all_to_all(planned_density, "dp", split_axis=0, concat_axis=0, tiled=True),
        "sub",
        split_axis=1,
        concat_axis=1,
        tiled=True,
    )
    back_spread = lax.all_to_all(spread_density, "dp", split_axis=0, concat_axis=0, tiled=True)
    from_planned = jnp.take(back_planned.reshape(-1), small_slot, mode="clip")
    from_spread = jnp.take(back_spread.reshape(-1), large_slot, mode="clip")
    return jnp.where(planned, from_planned, from_spread)


def solution(mesh):
    placed = (P(("dp", "sub"), None), P(("dp", "sub")))
    return jax.shard_map(
        local, mesh=mesh, in_specs=placed, out_specs=P(("dp", "sub")), check_vma=False
    )
```

profile of v0, /device:TPU:1, one launch (start us, length us, event | category | flops | bytes accessed | tf_op | source)
XLA Modules:
  0.0 422.4 jit_solution(3138771682105180316)
XLA Ops:
  8.6 4.5 %scatter_custom_fusion.2 = s32[256]{0:T(256)S(1)} fusion(s32[1024]{0:T(1024)S(1)} %get-tuple-element.88, s32[1024]{0:T(1024)} %param.5, s32[]{:T(128)} %constant.92.clone.1), kind=kCustom, calls=%fused_computation.76 | custom fusion | bytes 1536 | tf_op jit(solution)/shard_map/scatter | solution.py:85
  13.8 19.3 %all-to-all-start.6 = ((s32[64,1,4]{2,1,0:T(1,128)}), s32[64,1,4]{2,1,0:T(1,128)S(1)}, u32[]{:S(2)}, u32[]{:S(2)}) async-start(s32[64,1,4]{2,1,0:T(1,128)} %bitcast), calls=%async_computation.6 | async-start | bytes 65536 | tf_op jit(solution)/shard_map/all_to_all | solution.py:106
  35.7 4.5 %scatter_custom_fusion = s32[1536]{0:T(1024)S(1)} fusion(s32[1024]{0:T(1024)S(1)} %get-tuple-element.90, s32[1024]{0:T(1024)} %param.5, s32[]{:T(128)} %constant.92.clone.1), kind=kCustom, calls=%fused_computation.63 | custom fusion | bytes 6656 | tf_op jit(solution)/shard_map/scatter | solution.py:75
  41.5 5.2 %all-to-all-done.6 = s32[64,1,4]{2,1,0:T(1,128)S(1)} async-done(((s32[64,1,4]{2,1,0:T(1,128)}), s32[64,1,4]{2,1,0:T(1,128)S(1)}, u32[]{:S(2)}, u32[]{:S(2)}) %all-to-all-start.6) | async-done | bytes 1056 | tf_op jit(solution)/shard_map/all_to_all | solution.py:106
  46.7 9.3 %all-to-all-start = ((s32[64,8,3]{1,2,0:T(4,128)}), s32[64,8,3]{1,2,0:T(4,128)S(1)}, u32[]{:S(2)}, u32[]{:S(2)}) async-start(s32[64,8,3]{1,2,0:T(4,128)} %copy.16), calls=%async_computation | async-start | bytes 262144 | tf_op jit(solution)/shard_map/all_to_all | solution.py:97
  56.0 5.7 %scatter_custom_fusion.3 = bf16[256,1024]{1,0:T(8,128)(2,1)S(1)} fusion(s32[1024]{0:T(1024)S(1)} %get-tuple-element.88, bf16[1024,1024]{1,0:T(8,128)(2,1)S(1)} %copy-done, f32[1024]{0:T(1024)S(1)} %add_rsqrt_fusion, bf16[]{:T(256)} %constant.90.clone.1), kind=kCustom, calls=%fused_computation.40 | custom fusion | flops 3145728 | bytes 2625538 | tf_op jit(solution)/shard_map/scatter | solution.py:81
  62.7 8.4 %all-to-all-done = s32[64,8,3]{1,2,0:T(4,128)S(1)} async-done(((s32[64,8,3]{1,2,0:T(4,128)}), s32[64,8,3]{1,2,0:T(4,128)S(1)}, u32[]{:S(2)}, u32[]{:S(2)}) %all-to-all-start) | async-done | bytes 6176 | tf_op jit(solution)/shard_map/all_to_all | solution.py:97
  71.1 6.4 %all-to-all-start.7 = ((bf16[64,4,1024]{2,1,0:T(4,128)(2,1)}), bf16[64,4,1024]{2,1,0:T(4,128)(2,1)S(1)}, u32[]{:S(2)}, u32[]{:S(2)}) async-start(bf16[64,4,1024]{2,1,0:T(4,128)(2,1)} %reshape.104), calls=%async_computation.7 | async-start | bytes 1048576 | tf_op jit(solution)/shard_map/all_to_all | solution.py:105
  77.5 7.8 %scatter_custom_fusion.1 = bf16[1536,1024]{1,0:T(8,128)(2,1)} fusion(s32[1024]{0:T(1024)S(1)} %get-tuple-element.90, bf16[]{:T(256)} %constant.90.clone.1, bf16[1024,1024]{1,0:T(8,128)(2,1)S(1)} %copy-done, f32[1024]{0:T(1024)S(1)} %add_rsqrt_fusion), kind=kCustom, calls=%fused_computation.37 | custom fusion | flops 3145728 | bytes 5246978 | tf_op jit(solution)/shard_map/scatter | solution.py:69
  85.3 9.1 %reshape.100 = bf16[64,8,3,1024]{3,2,1,0:T(4,128)(2,1)} reshape(bf16[1536,1024]{1,0:T(8,128)(2,1)} %scatter_custom_fusion.1) | data formatting | bytes 6291456 | tf_op jit(solution)/shard_map/reshape | solution.py:71
  94.4 5.6 %copy.19 = bf16[64,8,3,1024]{3,1,2,0:T(8,128)(2,1)} copy(bf16[64,8,3,1024]{3,2,1,0:T(4,128)(2,1)} %reshape.100) | data formatting | bytes 6291456 | tf_op jit(solution)/shard_map/reshape | solution.py:71
  100.0 6.3 %all-to-all-done.7 = bf16[64,4,1024]{2,1,0:T(4,128)(2,1)S(1)} async-done(((bf16[64,4,1024]{2,1,0:T(4,128)(2,1)}), bf16[64,4,1024]{2,1,0:T(4,128)(2,1)S(1)}, u32[]{:S(2)}, u32[]{:S(2)}) %all-to-all-start.7) | async-done | bytes 524320 | tf_op jit(solution)/shard_map/all_to_all | solution.py:105
  107.0 8.9 %all-to-all-start.2 = ((bf16[64,8,3,1024]{3,1,2,0:T(8,128)(2,1)}), bf16[64,8,3,1024]{3,1,2,0:T(8,128)(2,1)S(1)}, u32[]{:S(2)}, u32[]{:S(2)}) async-start(bf16[64,8,3,1024]{3,1,2,0:T(8,128)(2,1)} %copy.19), calls=%async_computation.2 | async-start | bytes 6291456 | tf_op jit(solution)/shard_map/all_to_all | solution.py:90
  118.8 135.5 %all-to-all-done.2 = bf16[64,8,3,1024]{3,1,2,0:T(8,128)(2,1)S(1)} async-done(((bf16[64,8,3,1024]{3,1,2,0:T(8,128)(2,1)}), bf16[64,8,3,1024]{3,1,2,0:T(8,128)(2,1)S(1)}, u32[]{:S(2)}, u32[]{:S(2)}) %all-to-all-start.2) | async-done | bytes 3145760 | tf_op jit(solution)/shard_map/all_to_all | solution.py:90
  254.3 12.1 %all-to-all-start.1 = ((s32[8,1,192]{2,1,0:T(1,128)}), s32[8,1,192]{2,1,0:T(1,128)S(1)}, u32[]{:S(2)}, u32[]{:S(2)}) async-start(s32[8,1,192]{2,1,0:T(1,128)} %reshape.193), calls=%async_computation.1 | async-start | bytes 16384 | tf_op jit(solution)/shard_map/all_to_all | solution.py:96
  266.4 3.4 copy.20
  271.0 4.3 %all-to-all-start.3 = ((bf16[64,8,3,1024]{3,0,2,1:T(8,128)(2,1)}), bf16[64,8,3,1024]{3,0,2,1:T(8,128)(2,1)S(1)}, u32[]{:S(2)}, u32[]{:S(2)}) async-start(bf16[64,8,3,1024]{3,0,2,1:T(8,128)(2,1)} %copy.20), calls=%async_computation.3 | async-start | bytes 6291456 | tf_op jit(solution)/shard_map/all_to_all | solution.py:89
  276.7 39.7 %all-gather = s32[8,1,256]{2,1,0:T(1,128)S(1)} all-gather(s32[1,1,256]{2,1,0:T(1,128)S(1)} %reshape.161), channel_id=1, replica_groups=mesh['dp'=64,'sub'=8] {'sub'}, dimensions={0}, use_global_device_ids=true | all-gather | bytes 9216 | tf_op jit(solution)/shard_map/all_gather | solution.py:132
  318.9 4.2 %fusion.18 = f32[256]{0:T(256)S(1)} fusion(bf16[256,1024]{1,0:T(8,128)(2,1)} %reshape.105, bf16[2048,1024]{1,0:T(8,128)(2,1)} %all-gather.3.cloned.1.call-done, s32[256]{0:T(256)S(1)} %iota_add_fusion.1, s32[2048]{0:T(1024)S(1)} %bitcast.31, s32[256]{0:T(256)S(1)} %eq.64, pred[256]{0:T(512)(128)(4,1)S(1)} %broadcast_compare_fusion.2), kind=kOutput, calls=%fused_computation.39 | convolution fusion | flops 1077411584 | bytes 4730112 | tf_op jit(solution)/shard_map/dot_general | solution.py:20
  323.3 4.6 %copy.21 = bf16[64,8,3,1024]{3,2,1,0:T(4,128)(2,1)} copy(bf16[64,8,3,1024]{3,0,2,1:T(8,128)(2,1)S(1)} %all-to-all-done.3) | data formatting | bytes 6291456 | tf_op jit(solution)/shard_map/all_to_all | solution.py:89
  327.9 7.5 %reshape.101 = bf16[1536,1024]{1,0:T(8,128)(2,1)S(1)} reshape(bf16[64,8,3,1024]{3,2,1,0:T(4,128)(2,1)} %copy.21) | data formatting | bytes 6291456 | tf_op jit(solution)/shard_map/reshape | solution.py:108
  335.4 15.6 %while.12 = (s32[]{:T(128)}, f32[3,512]{1,0:T(4,128)S(1)}, s32[3]{0:T(128)S(1)}, s32[1536]{0:T(1024)S(1)}, s32[64,8,3]{2,1,0:T(8,128)}, /*index=5*/bf16[1536,102...) while((s32[]{:T(128)}, f32[3,512]{1,0:T(4,128)S(1)}, ...), condition=%wide.wide.region_7.8_spmd.clone, body=%wide.wide.region_4.7_spmd.clone.sunk | while | flops 1619265024 | bytes 4237495 | solution.py:124
  337.6 3.0 fusion.48
  342.8 3.0 fusion.48
  348.0 3.0 fusion.48
  352.3 5.6 %all-to-all-start.4 = ((f32[64,8,3]{1,2,0:T(4,128)}), f32[64,8,3]{1,2,0:T(4,128)S(1)}, u32[]{:S(2)}, u32[]{:S(2)}) async-start(f32[64,8,3]{1,2,0:T(4,128)} %copy.23), calls=%async_computation.4 | async-start | bytes 262144 | tf_op jit(solution)/shard_map/all_to_all | solution.py:141
  358.5 15.0 %all-to-all-done.4 = f32[64,8,3]{1,2,0:T(4,128)S(1)} async-done(((f32[64,8,3]{1,2,0:T(4,128)}), f32[64,8,3]{1,2,0:T(4,128)S(1)}, u32[]{:S(2)}, u32[]{:S(2)}) %all-to-all-start.4) | async-done | bytes 6176 | tf_op jit(solution)/shard_map/all_to_all | solution.py:141
  373.5 5.8 %all-to-all-start.8 = ((f32[64,1,4]{2,1,0:T(1,128)}), f32[64,1,4]{2,1,0:T(1,128)S(1)}, u32[]{:S(2)}, u32[]{:S(2)}) async-start(f32[64,1,4]{2,1,0:T(1,128)} %bitcast.3), calls=%async_computation.8 | async-start | bytes 65536 | tf_op jit(solution)/shard_map/all_to_all | solution.py:147
  380.1 12.8 %all-to-all-done.8 = f32[64,1,4]{2,1,0:T(1,128)S(1)} async-done(((f32[64,1,4]{2,1,0:T(1,128)}), f32[64,1,4]{2,1,0:T(1,128)S(1)}, u32[]{:S(2)}, u32[]{:S(2)}) %all-to-all-start.8) | async-done | bytes 1056 | tf_op jit(solution)/shard_map/all_to_all | solution.py:147
  392.9 6.0 %all-to-all-start.5 = ((f32[8,1,192]{2,1,0:T(1,128)}), f32[8,1,192]{2,1,0:T(1,128)S(1)}, u32[]{:S(2)}, u32[]{:S(2)}) async-start(f32[8,1,192]{2,1,0:T(1,128)} %reshape.195), calls=%async_computation.5 | async-start | bytes 16384 | tf_op jit(solution)/shard_map/all_to_all | solution.py:140
  400.3 6.8 %gather_fusion.1 = f32[1024]{0:T(1024)S(1)} fusion(f32[256]{0:T(256)S(1)} %reshape.106, s32[1024]{0:T(1024)S(1)} %get-tuple-element.87), kind=kCustom, calls=%fused_computation.1 | custom fusion | bytes 12288 | tf_op jit(solution)/shard_map/jit(_take)/gather | solution.py:149
  408.8 6.2 %gather_fusion = f32[1024]{0:T(1024)S(1)} fusion(f32[1536]{0:T(1024)S(1)} %reshape.103, s32[1024]{0:T(1024)S(1)} %get-tuple-element.89), kind=kCustom, calls=%fused_computation | custom fusion | bytes 12288 | tf_op jit(solution)/shard_map/jit(_take)/gather | solution.py:148
  (75 shorter events, 27.1 us)
Async XLA Ops:
  6.5 49.5 %copy-start = (bf16[1024,1024]{1,0:T(8,128)(2,1)S(1)}, bf16[1024,1024]{1,0:T(8,128)(2,1)}, u32[]{:S(2)}) copy-start(bf16[1024,1024]{1,0:T(8,128)(2,1)} %param.4) | copy-start | bytes 6291460
  13.8 32.9 %all-to-all-start.6 = ((s32[64,1,4]{2,1,0:T(1,128)}), s32[64,1,4]{2,1,0:T(1,128)S(1)}, u32[]{:S(2)}, u32[]{:S(2)}) async-start(s32[64,1,4]{2,1,0:T(1,128)} %bitcast), calls=%async_computation.6 | async-start | bytes 65536 | tf_op jit(solution)/shard_map/all_to_all | solution.py:106
  46.7 24.4 %all-to-all-start = ((s32[64,8,3]{1,2,0:T(4,128)}), s32[64,8,3]{1,2,0:T(4,128)S(1)}, u32[]{:S(2)}, u32[]{:S(2)}) async-start(s32[64,8,3]{1,2,0:T(4,128)} %copy.16), calls=%async_computation | async-start | bytes 262144 | tf_op jit(solution)/shard_map/all_to_all | solution.py:97
  71.1 35.1 %all-to-all-start.7 = ((bf16[64,4,1024]{2,1,0:T(4,128)(2,1)}), bf16[64,4,1024]{2,1,0:T(4,128)(2,1)S(1)}, u32[]{:S(2)}, u32[]{:S(2)}) async-start(bf16[64,4,1024]{2,1,0:T(4,128)(2,1)} %reshape.104), calls=%async_computation.7 | async-start | bytes 1048576 | tf_op jit(solution)/shard_map/all_to_all | solution.py:105
  106.2 0.8 copy-start.2
  107.0 147.2 %all-to-all-start.2 = ((bf16[64,8,3,1024]{3,1,2,0:T(8,128)(2,1)}), bf16[64,8,3,1024]{3,1,2,0:T(8,128)(2,1)S(1)}, u32[]{:S(2)}, u32[]{:S(2)}) async-start(bf16[64,8,3,1024]{3,1,2,0:T(8,128)(2,1)} %copy.19), calls=%async_computation.2 | async-start | bytes 6291456 | tf_op jit(solution)/shard_map/all_to_all | solution.py:90
  116.0 202.9 %all-gather.3.cloned.1.call-start = ((), (), s32[]{:S(2)}) async-start(), calls=%async_computation.9 | async-start | bytes 4718592 | tf_op jit(solution)/shard_map/all_gather | solution.py:131
  254.3 16.7 %all-to-all-start.1 = ((s32[8,1,192]{2,1,0:T(1,128)}), s32[8,1,192]{2,1,0:T(1,128)S(1)}, u32[]{:S(2)}, u32[]{:S(2)}) async-start(s32[8,1,192]{2,1,0:T(1,128)} %reshape.193), calls=%async_computation.1 | async-start | bytes 16384 | tf_op jit(solution)/shard_map/all_to_all | solution.py:96
  271.0 52.3 %all-to-all-start.3 = ((bf16[64,8,3,1024]{3,0,2,1:T(8,128)(2,1)}), bf16[64,8,3,1024]{3,0,2,1:T(8,128)(2,1)S(1)}, u32[]{:S(2)}, u32[]{:S(2)}) async-start(bf16[64,8,3,1024]{3,0,2,1:T(8,128)(2,1)} %copy.20), calls=%async_computation.3 | async-start | bytes 6291456 | tf_op jit(solution)/shard_map/all_to_all | solution.py:89
  318.5 4.7 %copy-start.1 = (s32[64,8,3]{2,1,0:T(8,128)}, s32[64,8,3]{2,1,0:T(8,128)S(1)}, u32[]{:S(2)}) copy-start(s32[64,8,3]{2,1,0:T(8,128)S(1)} %copy.18) | copy-start | bytes 18436
  352.3 21.2 %all-to-all-start.4 = ((f32[64,8,3]{1,2,0:T(4,128)}), f32[64,8,3]{1,2,0:T(4,128)S(1)}, u32[]{:S(2)}, u32[]{:S(2)}) async-start(f32[64,8,3]{1,2,0:T(4,128)} %copy.23), calls=%async_computation.4 | async-start | bytes 262144 | tf_op jit(solution)/shard_map/all_to_all | solution.py:141
  373.5 19.4 %all-to-all-start.8 = ((f32[64,1,4]{2,1,0:T(1,128)}), f32[64,1,4]{2,1,0:T(1,128)S(1)}, u32[]{:S(2)}, u32[]{:S(2)}) async-start(f32[64,1,4]{2,1,0:T(1,128)} %bitcast.3), calls=%async_computation.8 | async-start | bytes 65536 | tf_op jit(solution)/shard_map/all_to_all | solution.py:147
  392.9 14.2 %all-to-all-start.5 = ((f32[8,1,192]{2,1,0:T(1,128)}), f32[8,1,192]{2,1,0:T(1,128)S(1)}, u32[]{:S(2)}, u32[]{:S(2)}) async-start(f32[8,1,192]{2,1,0:T(1,128)} %reshape.195), calls=%async_computation.5 | async-start | bytes 16384 | tf_op jit(solution)/shard_map/all_to_all | solution.py:140
Sparse Core Ops, SparseCore 0:
  119.0 42.0 all-gather.2
where the time goes:
time: 424 us; the launch traced here: 422 us
  waiting for transfers between devices  184 us (43%)
  starting transfers between devices  77.6 us (18%)
  local copies, waits for them, and re-layouts  66.6 us (16%)
  blocking collectives  39.7 us (9%)
  other arithmetic  24.9 us (6%)
  between operations  13.7 us (3%)
  matrix products  13.3 us (3%)
    all_to_all x1, waiting for transfers between devices, local(): lax.all_to_all(small_send, 'dp', split_axis=0, concat_axis=0, tiled=True)  136 us
    all_gather x1, blocking collectives, local(): piece_ids = lax.all_gather(spread_ids, 'sub', axis=0, tiled=True)  39.7 us
    all_to_all x1, starting transfers between devices, local(): lax.all_to_all(large_tags, 'dp', split_axis=0, concat_axis=0, tiled=True)  19.3 us
    all_to_all x1, waiting for transfers between devices, local(): lax.all_to_all(planned_density, 'dp', split_axis=0, concat_axis=0, tiled=...  15 us
    reshape x2, local copies, waits for them, and re-layouts, local(): small_send.reshape(dp_count, sub_count, small_cap, feature_width)  14.7 us
    dot_general x4, matrix products, pair_terms(): lax.dot_general(left_rows, right_rows, (((1,), (1,)), ((), ())), preferre...  13.3 us
    all_to_all x1, waiting for transfers between devices, local(): lax.all_to_all(spread_density, 'dp', split_axis=0, concat_axis=0, tiled=T...  12.8 us
    all_to_all x1, starting transfers between devices, local(): lax.all_to_all(lax.all_to_all(small_tags, 'dp', split_axis=0, concat_axis...  12.1 us
  transfers between devices with their start and end apart: 10, of which 7 were waited for; matrix products, arithmetic and copies ran while one was open for 15% of the time, Pallas kernels for 0%

commit v1 on v0

v1 whole, which is shorter than its diff:
```python
import functools

import jax
import jax.numpy as jnp
from jax import lax
from jax.experimental import pallas as pl
from jax.experimental.pallas import tpu as pltpu
from jax.sharding import PartitionSpec as P

MESH = pl.DeviceIdType.MESH
F32 = jnp.float32
BF16 = jnp.bfloat16
I32 = jnp.int32
NZ = 16
NY = 4
NS = 8
ND = NY * NS
MSG = 128
SCALE = 32.0


def iota(shape, axis):
    return lax.broadcasted_iota(I32, shape, axis)


def nn(left, right, precision=None):
    return lax.dot_general(
        left, right, (((1,), (0,)), ((), ())), precision=precision, preferred_element_type=F32
    )


def nt(left, right, precision=None):
    return lax.dot_general(
        left, right, (((1,), (1,)), ((), ())), precision=precision, preferred_element_type=F32
    )


def exact_nn(left, right):
    return nn(left, right, lax.Precision.HIGHEST)


def exact_nt(left, right):
    return nt(left, right, lax.Precision.HIGHEST)


def hot(condition, dtype=BF16):
    return jnp.where(condition, 1.0, 0.0).astype(dtype)


def step_of(message):
    place = message + 1
    return lax.rem(8 + (place // 2) * (2 * lax.rem(place, 2) - 1) + NZ, NZ)


def kernel(
    cap,
    x_ref,
    g_ref,
    tag_ref,
    v_ref,
    unit,
    send,
    recv,
    trecv,
    out_w,
    out_s,
    fin_w,
    fin_s,
    own,
    row_acc,
    col_acc,
    kinds,
    s_valid,
    back_a,
    got_a,
    back_b,
    got_b,
    z_send,
    z_recv,
    t_send,
    t_recv,
    w_send,
    w_recv,
    s_send,
    s_recv,
    a_sem,
    b_sem,
):
    dp = lax.axis_index("dp")
    sub = lax.axis_index("sub")
    z = dp // NY
    y = lax.rem(dp, NY)
    me = y * NS + sub

    def z_peer(step):
        return (lax.rem(z + step + NZ, NZ) * NY + y, sub)

    def plane_peer(d):
        return (z * NY + d // NS, lax.rem(d, NS))

    barrier = pltpu.get_barrier_semaphore()

    @pl.loop(1, NZ)
    def _(i):
        pl.semaphore_signal(barrier, inc=1, device_id=z_peer(i), device_id_type=MESH)

    @pl.loop(1, ND)
    def _(i):
        pl.semaphore_signal(
            barrier, inc=1, device_id=plane_peer(lax.rem(me + i, ND)), device_id_type=MESH
        )

    @pl.loop(0, 8)
    def _(i):
        rows = pl.ds(pl.multiple_of(i * 128, 128), 128)
        floats = x_ref[rows, :].astype(F32)
        total = jnp.sum(floats * floats, axis=1, keepdims=True)
        unit[rows, :] = (floats * lax.rsqrt(total + 1e-06)).astype(BF16)

    if cap < MSG:

        @pl.loop(0, NZ)
        def _(m):
            recv[m, cap:, :] = jnp.zeros((MSG - cap, 1024), BF16)

    pl.semaphore_wait(barrier, NZ - 1 + ND - 1)

    def z_copy(m):
        return pltpu.make_async_remote_copy(
            src_ref=send.at[m],
            dst_ref=recv.at[m, pl.ds(0, cap)],
            send_sem=z_send.at[m],
            recv_sem=z_recv.at[m],
            device_id=z_peer(step_of(m)),
            device_id_type=MESH,
        )

    def tag_copy(m):
        part = pl.ds(pl.multiple_of(m * 8, 8), 8)
        return pltpu.make_async_remote_copy(
            src_ref=tag_ref.at[part],
            dst_ref=trecv.at[part],
            send_sem=t_send.at[m],
            recv_sem=t_recv.at[m],
            device_id=z_peer(step_of(m)),
            device_id_type=MESH,
        )

    @pl.loop(0, NZ)
    def _(m):
        pick = hot(iota((cap, 1024), 0) + m * MSG == g_ref[...])
        rows = nn(pick, unit[...]).astype(BF16)

        @pl.when(m < NZ - 1)
        def _():
            send[m] = rows
            z_copy(m).start()
            tag_copy(m).start()

        @pl.when(m == NZ - 1)
        def _():
            recv[m, :cap, :] = rows
            trecv[(NZ - 1) * 8 :, :] = tag_ref[(NZ - 1) * 8 :, :]

    def part_of(d):
        return pl.ds(pl.multiple_of(d * 16, 16), 16)

    def w_copy(c, d):
        return pltpu.make_async_remote_copy(
            src_ref=out_w.at[c, part_of(d)],
            dst_ref=fin_w.at[c, part_of(me)],
            send_sem=w_send.at[c],
            recv_sem=w_recv.at[c],
            device_id=plane_peer(d),
            device_id_type=MESH,
        )

    def s_copy(c, d):
        return pltpu.make_async_remote_copy(
            src_ref=out_s.at[c, part_of(d // NS)],
            dst_ref=fin_s.at[c, part_of(me)],
            send_sem=s_send.at[c],
            recv_sem=s_recv.at[c],
            device_id=plane_peer(d),
            device_id_type=MESH,
        )

    def wait_all(ref, sem):
        pltpu.make_async_copy(ref, ref, sem).wait()

    def forward(c):
        for j in range(4):
            m = c * 4 + j

            @pl.when(m < NZ - 1)
            def _():
                z_copy(m).wait_recv()
                tag_copy(m).wait_recv()

        tags = trecv[pl.ds(pl.multiple_of(c * 32, 32), 32), :]
        tags = jnp.concatenate([tags[8 * j : 8 * j + 1] for j in range(4)], axis=1)
        value = tags.astype(I32) - 1
        lane = iota((1, 4 * MSG), 1)
        source = lane // MSG
        kind = (value & 1) + 1
        code = value >> 1
        rank = code & 3
        is_spread = code >= 4 * ND
        is_whole = (code >= 0) & (code < 4 * ND)
        w_dev = jnp.where(is_whole, code >> 2, -1)
        w_slot = source * 3 + rank
        s_dev = jnp.where(is_spread, (code >> 2) - ND, -1)
        s_slot = source * 4 + rank
        place = jnp.where(
            is_whole,
            w_dev * 16 + w_slot,
            jnp.where(is_spread, ND * 16 + s_dev * 16 + s_slot, -1),
        )
        pick = hot(iota((ND * 16 + NY * 16, 4 * MSG), 0) == place)
        w_kind = jnp.where(iota((ND, 4 * MSG), 0) == w_dev, kind, 0).astype(F32).astype(BF16)
        w_tags = nt(w_kind, hot(iota((128, 4 * MSG), 0) == w_slot))
        s_tags = nt(
            hot(iota((ND, 4 * MSG), 0) // NS == s_dev),
            hot(iota((128, 4 * MSG), 0) == s_slot),
        )
        line = iota((ND * 16, ND), 0)
        where_w = hot(line == iota((ND * 16, ND), 1) * 16 + 12)
        where_s = hot(line == iota((ND * 16, ND), 1) * 16 + 13)
        extra = nn(where_w, w_tags.astype(BF16)) + nn(where_s, s_tags.astype(BF16))
        rows = recv.at[pl.ds(c * 4, 4)]
        for n in range(4):
            cols = pl.ds(n * 256, 256)
            block = rows[:, :, cols].reshape(4 * MSG, 256)
            picked = nn(pick, block)
            whole = picked[: ND * 16]
            if n == 0:
                whole = jnp.concatenate([whole[:, :128] + extra, whole[:, 128:]], axis=1)
            out_w[c, :, cols] = whole.astype(BF16)
            out_s[c, :, cols] = picked[ND * 16 :].astype(BF16)

        @pl.loop(1, ND)
        def _(i):
            d = lax.rem(me + i, ND)
            w_copy(c, d).start()
            s_copy(c, d).start()

        fin_w[c, part_of(me), :] = out_w[c, part_of(me), :]
        fin_s[c, part_of(me), :] = out_s[c, part_of(y), :]

    def tags_of(c):
        line = iota((2 * ND, ND * 16), 1)
        head = iota((2 * ND, ND * 16), 0)
        want = jnp.where(head < ND, head * 16 + 12, (head - ND) * 16 + 13)
        return nn(hot(line == want), fin_w[c, :, 0:128])

    def as_rows(tags):
        line = iota((ND * 16, ND), 0)
        spread = nn(hot(line // 16 == iota((ND * 16, ND), 1)), tags.astype(BF16))
        keep = iota((ND * 16, 128), 1) == lax.rem(iota((ND * 16, 128), 0), 16)
        return jnp.sum(jnp.where(keep, spread, 0.0), axis=1, keepdims=True)

    def as_lanes(tags):
        spread = nn(
            tags.astype(BF16), hot(iota((128, ND * 16), 0) == lax.rem(iota((128, ND * 16), 1), 16))
        )
        keep = iota((ND, ND * 16), 0) == iota((ND, ND * 16), 1) // 16
        return jnp.sum(jnp.where(keep, spread, 0.0), axis=0, keepdims=True)

    def compute(c):
        wait_all(fin_w.at[c, pl.ds(0, (ND - 1) * 16)], w_recv.at[c])
        wait_all(fin_s.at[c, pl.ds(0, (ND - 1) * 16)], s_recv.at[c])
        tags = tags_of(c)
        w_tags = tags[:ND]
        kinds[:, pl.ds(0, 128)] += nn(
            w_tags.astype(BF16), hot(iota((128, 128), 1) == iota((128, 128), 0) + c * 16)
        )
        row_acc[c, :, 1:2] = as_rows(w_tags)
        s_valid[c, :, 0:1] = as_rows(tags[ND:])
        lanes = as_lanes(w_tags)
        lanes = jnp.where(lanes > 0.0, lanes, -1.0)
        right = fin_w[c]

        @pl.loop(0, c + 1)
        def _(b):
            similar = nt(fin_w[b], right)
            same = row_acc[b, :, 1:2] == lanes
            other = (iota((ND * 16, ND * 16), 0) != iota((ND * 16, ND * 16), 1)) | (b != c)
            weights = jnp.where(same & other, jnp.exp(SCALE * similar), 0.0)
            col_acc[c] += jnp.broadcast_to(
                jnp.sum(weights, axis=0, keepdims=True), (8, ND * 16)
            )

            @pl.when(b != c)
            def _():
                row_acc[b, :, 0:1] += jnp.sum(weights, axis=1, keepdims=True)

    kinds[...] = jnp.zeros_like(kinds)
    row_acc[...] = jnp.zeros_like(row_acc)
    col_acc[...] = jnp.zeros_like(col_acc)

    @pl.loop(0, 5)
    def _(c):
        @pl.when(c < 4)
        def _():
            forward(c)

        @pl.when(c > 0)
        def _():
            compute(c - 1)

    for c in range(4):
        for j in range(NY):
            own[c * 64 + j * 16 : c * 64 + j * 16 + 16, :] = fin_s[c, part_of(j * NS + sub), :]
    own_rows = own[...]
    lane = iota((1, 256), 1)
    own_chunk = lane // 64
    own_line = (lax.rem(lane, 64) // 16 * NS + sub) * 16 + lax.rem(lane, 16)
    s_mass = jnp.zeros((1, 256), F32)
    s_count = jnp.zeros((1, 1), F32)
    for c in range(4):
        similar = nt(fin_s[c], own_rows)
        valid = s_valid[c, :, 0:1]
        self_pair = (own_chunk == c) & (iota((ND * 16, 256), 0) == own_line)
        weights = jnp.where((valid > 0.0) & ~self_pair, jnp.exp(SCALE * similar), 0.0)
        s_mass += jnp.sum(weights, axis=0, keepdims=True)
        s_count += jnp.sum(valid, axis=0, keepdims=True)
    s_density = s_mass / jnp.maximum(s_count, 1.0)

    mass = jnp.zeros((ND, 128), F32)
    device_of = iota((ND, ND * 16), 1) // 16 == iota((ND, ND * 16), 0)
    for c in range(4):
        to_lane = iota((ND * 16, 128), 1) == c * 16 + lax.rem(iota((ND * 16, 128), 0), 16)
        placed = jnp.where(to_lane, row_acc[c, :, 0:1], 0.0)
        mass += jnp.sum(placed.reshape(ND, 16, 128), axis=1)
        masked = jnp.where(device_of, col_acc[c, 0:1, :], 0.0)
        mass += exact_nt(
            masked,
            hot(iota((128, ND * 16), 0) == c * 16 + lax.rem(iota((128, ND * 16), 1), 16), F32),
        )
    kind = kinds[...]
    first = jnp.sum(hot(kind == 1.0, F32), keepdims=True)
    second = jnp.sum(hot(kind == 2.0, F32), keepdims=True)
    density = jnp.where(
        kind > 0.0, mass / jnp.maximum(jnp.where(kind == 1.0, first, second), 1.0), 0.0
    )
    own_of = iota((ND, 256), 0) == lax.rem(iota((ND, 256), 1), 64) // 16 * NS + sub
    density += exact_nt(
        jnp.where(own_of, s_density, 0.0),
        hot(
            iota((128, 256), 0)
            == 64 + iota((128, 256), 1) // 64 * 16 + lax.rem(iota((128, 256), 1), 16),
            F32,
        ),
    )
    back_a[...] = exact_nn(hot(iota((ND * 8, ND), 0) // 8 == iota((ND * 8, ND), 1), F32), density)

    def lines_of(i):
        return pl.ds(pl.multiple_of(i * 8, 8), 8)

    @pl.loop(1, ND)
    def _(i):
        d = lax.rem(me + i, ND)
        pltpu.make_async_remote_copy(
            src_ref=back_a.at[lines_of(d)],
            dst_ref=got_a.at[lines_of(me)],
            send_sem=a_sem.at[0],
            recv_sem=a_sem.at[1],
            device_id=plane_peer(d),
            device_id_type=MESH,
        ).start()

    got_a[lines_of(me), :] = back_a[lines_of(me), :]
    wait_all(got_a.at[pl.ds(0, (ND - 1) * 8)], a_sem.at[1])
    lines = exact_nn(hot(iota((128, ND * 8), 1) == iota((128, ND * 8), 0) * 8, F32), got_a[...])
    head = iota((128, 128), 0)
    message = head // 8
    slot = lax.rem(head, 8)
    base = message // 4 * 16
    inner = lax.rem(message, 4)
    want = jnp.where(slot < 3, base + inner * 3 + slot, 64 + base + inner * 4 + slot - 3)
    want = jnp.where(slot < 7, want, -1)
    back_b[...] = exact_nt(hot(iota((128, 128), 1) == want, F32), lines)

    @pl.loop(0, NZ - 1)
    def _(m):
        pltpu.make_async_remote_copy(
            src_ref=back_b.at[lines_of(m)],
            dst_ref=got_b.at[lines_of(m)],
            send_sem=b_sem.at[0],
            recv_sem=b_sem.at[1],
            device_id=z_peer(NZ - step_of(m)),
            device_id_type=MESH,
        ).start()

    got_b[(NZ - 1) * 8 :, :] = back_b[(NZ - 1) * 8 :, :]
    wait_all(got_b.at[pl.ds(0, (NZ - 1) * 8)], b_sem.at[1])
    v_ref[...] = got_b[...]

    @pl.loop(0, NZ - 1)
    def _(m):
        z_copy(m).wait_send()
        tag_copy(m).wait_send()

    for c in range(4):
        wait_all(out_w.at[c, pl.ds(0, (ND - 1) * 16)], w_send.at[c])
        wait_all(fin_s.at[c, pl.ds(0, (ND - 1) * 16)], s_send.at[c])
    wait_all(back_a.at[pl.ds(0, (ND - 1) * 8)], a_sem.at[0])
    wait_all(back_b.at[pl.ds(0, (NZ - 1) * 8)], b_sem.at[0])


def exchange(cap, embeddings, spots, tags):
    vmem = pltpu.VMEM
    dma = pltpu.SemaphoreType.DMA
    return pl.pallas_call(
        functools.partial(kernel, cap),
        out_shape=jax.ShapeDtypeStruct((NZ * 8, 128), F32),
        in_specs=[pl.BlockSpec(memory_space=pltpu.VMEM)] * 3,
        out_specs=pl.BlockSpec(memory_space=pltpu.VMEM),
        scratch_shapes=[
            vmem((1024, 1024), BF16),
            vmem((NZ - 1, cap, 1024), BF16),
            vmem((NZ, MSG, 1024), BF16),
            vmem((NZ * 8, 128), F32),
            vmem((4, ND * 16, 1024), BF16),
            vmem((4, NY * 16, 1024), BF16),
            vmem((4, ND * 16, 1024), BF16),
            vmem((4, ND * 16, 1024), BF16),
            vmem((256, 1024), BF16),
            vmem((4, ND * 16, 128), F32),
            vmem((4, 8, ND * 16), F32),
            vmem((ND, 128), F32),
            vmem((4, ND * 16, 128), F32),
            vmem((ND * 8, 128), F32),
            vmem((ND * 8, 128), F32),
            vmem((NZ * 8, 128), F32),
            vmem((NZ * 8, 128), F32),
            dma((NZ,)),
            dma((NZ,)),
            dma((NZ,)),
            dma((NZ,)),
            dma((4,)),
            dma((4,)),
            dma((4,)),
            dma((4,)),
            dma((2,)),
            dma((2,)),
        ],
        compiler_params=pltpu.CompilerParams(
            collective_id=0, has_side_effects=True, vmem_limit_bytes=56 << 20
        ),
    )(embeddings, spots, tags)


def rank_within(labels):
    places = jnp.arange(labels.shape[0], dtype=I32)
    matches = (labels[:, None] == labels[None, :]) & (places[:, None] < places[None, :])
    return jnp.sum(matches.astype(I32), axis=0)


def local(embeddings, cluster_of):
    sub = lax.axis_index("sub")
    z = lax.axis_index("dp") // NY
    whole_count = 2 * NZ * ND
    whole = cluster_of < whole_count
    target = jnp.where(whole, cluster_of // 2, whole_count // 2 + cluster_of - whole_count)
    plane = jnp.where(whole, target // ND, (target - NZ * ND) // NY)
    rank = rank_within(target)
    spot = rank_within(plane)
    step = (plane - z + NZ) % NZ
    message = jnp.where(step >= 8, 2 * (step - 8), 2 * (8 - step) - 1)
    spots = message * MSG + spot
    device = jnp.where(whole, target % ND, (target - NZ * ND) % NY)
    code = jnp.where(whole, device * 4 + rank, 4 * ND + device * 4 + rank)
    value = 2 * code + jnp.where(whole, cluster_of % 2, 0) + 1
    slots = jnp.arange(NZ * MSG, dtype=I32)
    tags = jnp.sum(jnp.where(spots[None, :] == slots[:, None], value[None, :], 0), axis=1)
    tags = jnp.broadcast_to(tags.astype(F32).reshape(NZ, 1, MSG), (NZ, 8, MSG)).reshape(-1, MSG)
    cap = 112
    got = exchange(cap, embeddings, spots.reshape(1, -1), tags)
    line = message * 8 + jnp.where(whole, rank, 3 + rank)
    lane = jnp.where(whole, device, device * NS + sub)
    numbers = jnp.arange(128, dtype=I32)
    lines = nn(
        (line[:, None] == numbers[None, :]).astype(F32), got, lax.Precision.HIGHEST
    )
    return jnp.sum(jnp.where(lane[:, None] == numbers[None, :], lines, 0.0), axis=1)


def solution(mesh):
    placed = (P(("dp", "sub"), None), P(("dp", "sub")))
    return jax.shard_map(
        local, mesh=mesh, in_specs=placed, out_specs=P(("dp", "sub")), check_vma=False
    )
```

time: 424 us -> 267 us (0.63)
  Pallas kernels: 0 us -> 260 us
  waiting for transfers between devices: 184 us -> 0 us
  starting transfers between devices: 77.6 us -> 0 us
  local copies, waits for them, and re-layouts: 66.6 us -> 0.63 us
  blocking collectives: 39.7 us -> 0 us
  other arithmetic: 24.9 us -> 3.9 us
  between operations: 13.7 us -> 0.03 us
  matrix products: 13.3 us -> 2.03 us
    pallas_call x0 -> x1, Pallas kernels: none -> 260 us  [exchange(): pl.pallas_call(functools.partial(kernel, cap), out_shape=jax.ShapeDtypeSt...]
    all_to_all x9 -> x0, waiting for transfers between devices: 184 us -> none  [the longest x1 136 us: local(): lax.all_to_all(small_send, 'dp', split_axis=0, concat_axis=0, tiled=True)]
    all_to_all x9 -> x0, starting transfers between devices: 77.6 us -> none  [the longest x1 19.3 us: local(): lax.all_to_all(large_tags, 'dp', split_axis=0, concat_axis=0, tiled=True)]
    all_gather x1 -> x0, blocking collectives: 39.7 us -> none  [local(): piece_ids = lax.all_gather(spread_ids, 'sub', axis=0, tiled=True)]
    reshape x12 -> x1, local copies, waits for them, and re-layouts: 28.2 us -> 0.62 us  [local(): jnp.broadcast_to(tags.astype(F32).reshape(NZ, 1, MSG), (NZ, 8, MSG))]
    scatter x2 -> x0, other arithmetic: 13.5 us -> none  [the longest x1 7.81 us: local(): small_send = jnp.zeros((device_count * small_cap, feature_width), jnp.bfl...]
    gather x2 -> x0, local copies, waits for them, and re-layouts: 13 us -> none  [the longest x1 6.83 us: local(): from_spread = jnp.take(back_spread.reshape(-1), large_slot, mode='clip')]
    all_to_all x11 -> x0, local copies, waits for them, and re-layouts: 11.4 us -> none  [the longest x1 4.62 us: local(): lax.all_to_all(lax.all_to_all(small_send, 'dp', split_axis=0, concat_axis...]
  transfers between devices with their start and end apart: 10 -> 0, of which waited for: 7 -> 0; matrix products, arithmetic and copies ran while one was open for 15% -> 0% of each run, Pallas kernels for 0% -> 0%
where the time goes in v1:
time: 267 us; the launch traced here: 266 us
  Pallas kernels  260 us (97%)
  other arithmetic  3.9 us (1%)
    pallas_call x1, Pallas kernels, exchange(): pl.pallas_call(functools.partial(kernel, cap), out_shape=jax.ShapeDtypeSt...  260 us

profile of v1, /device:TPU:1, one launch (start us, length us, event | category | flops | bytes accessed | tf_op | source)
XLA Modules:
  0.0 266.4 jit_solution(15174249798500462222)
XLA Ops:
  0.0 0.7 add_select_fusion.9
  0.7 0.7 fusion.4
  1.4 0.4 convert_reduce_fusion.1
  1.8 0.7 fusion.8
  2.5 0.4 convert_reduce_fusion
  3.0 0.0 copy-start
  3.0 0.9 select_reduce_fusion
  3.9 0.6 broadcast_bitcast_fusion.tag_ref
  4.6 0.0 copy-done
  4.6 259.8 %shard_map.28 = f32[128,128]{1,0:T(8,128)} custom-call(bf16[1024,1024]{1,0:T(8,128)(2,1)} %x_ref.1, s32[1,1024]{1,0:T(1,128)} %bitcast.6, f32[128,128]{1,0:T(8,128)} %broadcast_bitcast_fusion.tag_ref), custom_call_target="tpu_custom_call" | custom-call | tf_op jit(solution)/shard_map/pallas_call | solution.py:414
  264.4 2.0 fusion.2
  (2 shorter events, 0.0 us)
Async XLA Ops:
  3.0 1.6 copy-start
